TPU v7x, 32 devices: a whole 2x2x4 slice. The times are simulated.
32 devices in a mesh: row: 8 (over y, x, core), col: 4 (over z).
Axes of the slice: x: 2, y: 2, z: 4, core: 2. Of those that a mesh axis runs over, the one named last changes fastest.
Arguments:
- front_matrix: bfloat16 [20480, 20480], P('row', 'col'), may hold values from -37 to 37
- right_samples: bfloat16 [20480, 256], P('col'), may hold values from -0.0390625 to 0.0390625
- left_samples: bfloat16 [20480, 256], P('row'), may hold values from -0.0390625 to 0.0390625
Outputs:
- residual: bfloat16 [20480, 20480], P('row', 'col')
- core_scaled: float32 [256, 256], replicated
All inputs are finite; a program needn't handle non-finite values.
Results may differ from a plain program's by a relative error of at most 0.0035.
Values may be sent and summed in bfloat16 or wider, within the bound.
A program may use at most 128 MiB of HBM per device.

v0:
```python
import jax
import jax.numpy as jnp
from jax import lax
from jax.sharding import PartitionSpec as P

ORDER = 20480


def gram_matrix(sketch):
    return lax.dot_general(
        sketch,
        sketch,
        (((0,), (0,)), ((), ())),
        precision=lax.Precision.HIGHEST,
        preferred_element_type=jnp.float32,
    )


def orthonormal(sketch, gram_total):
    lower_factor = jnp.linalg.cholesky(gram_total)
    return jax.scipy.linalg.solve_triangular(lower_factor, sketch.T, lower=True).T


def core_part(basis_rows, applied):
    return lax.dot_general(
        basis_rows.astype(jnp.float32),
        applied,
        (((0,), (0,)), ((), ())),
        precision=lax.Precision.HIGHEST,
        preferred_element_type=jnp.float32,
    )


def body(front_matrix, right_samples, left_samples):
    sketch_rows = jnp.dot(front_matrix, right_samples, preferred_element_type=jnp.float32)
    sketch_rows = lax.psum(sketch_rows, "col")
    sketch_cols = lax.dot_general(
        front_matrix, left_samples, (((0,), (0,)), ((), ())), preferred_element_type=jnp.float32
    )
    sketch_cols = lax.psum(sketch_cols, "row")
    gram_rows = lax.psum(gram_matrix(sketch_rows), "row")
    gram_cols = lax.psum(gram_matrix(sketch_cols), "col")
    basis_rows = orthonormal(sketch_rows, gram_rows).astype(jnp.bfloat16)
    basis_cols = orthonormal(sketch_cols, gram_cols).astype(jnp.bfloat16)
    applied = jnp.dot(front_matrix, basis_cols, preferred_element_type=jnp.float32)
    applied = lax.psum(applied, "col")
    core_matrix = lax.psum(core_part(basis_rows, applied), "row")
    core_scaled = core_matrix / jnp.sqrt(jnp.float32(ORDER))
    projected = jnp.dot(
        basis_rows.astype(jnp.float32),
        core_matrix,
        precision=lax.Precision.HIGHEST,
        preferred_element_type=jnp.float32,
    ).astype(jnp.bfloat16)
    update = lax.dot_general(
        projected, basis_cols, (((1,), (1,)), ((), ())), preferred_element_type=jnp.float32
    )
    residual = (front_matrix.astype(jnp.float32) - update).astype(jnp.bfloat16)
    return (residual, core_scaled)


def solution(mesh):
    in_specs = (P("row", "col"), P("col", None), P("row", None))
    out_specs = (P("row", "col"), P())
    return jax.shard_map(body, mesh=mesh, in_specs=in_specs, out_specs=out_specs, check_vma=False)
```

profile of v0, /device:TPU:0, one launch (start us, length us, event | category | flops | bytes accessed | tf_op | source)
XLA Modules:
  0.0 564.6 jit_solution(6918856674153980759)
XLA Ops:
  7.2 1.7 copy-done
  8.9 13.5 %fusion.23 = f32[2560,256]{1,0:T(8,128)} fusion(bf16[2560,5120]{1,0:T(8,128)(2,1)} %param.4, bf16[5120,256]{1,0:T(8,128)(2,1)S(1)} %copy-done), kind=kOutput, calls=%fused_computation.65 | convolution fusion | flops 6710886400 | bytes 31457280 | tf_op jit(solution)/shard_map/dot_general | solution.py:35
  23.8 15.1 %fusion.25 = f32[5120,256]{1,0:T(8,128)} fusion(bf16[2560,5120]{1,0:T(8,128)(2,1)} %param.4, bf16[2560,256]{1,0:T(8,128)(2,1)S(1)} %copy-done.10), kind=kOutput, calls=%fused_computation.67 | convolution fusion | flops 6710886400 | bytes 32768000 | tf_op jit(solution)/shard_map/dot_general | solution.py:37
  38.8 90.6 %all-reduce.8.cloned.1.call-done = f32[2560,256]{1,0:T(8,128)} async-done(((f32[2560,256]{1,0:T(8,128)}), f32[2560,256]{1,0:T(8,128)}) %all-reduce.8.cloned.1.call-update) | async-done | bytes 2621456 | tf_op jit(solution)/shard_map/psum | solution.py:36
  129.4 7.5 %fusion.24 = f32[256,256]{0,1:T(8,128)} fusion(f32[2560,256]{1,0:T(8,128)} %all-reduce.8.cloned.1.call-done), kind=kOutput, calls=%fused_computation.66 | convolution fusion | flops 2013265920 | bytes 2883584 | tf_op jit(solution)/shard_map/dot_general | solution.py:10
  137.2 94.2 %all-reduce.16.cloned.1.call-done = (f32[5120,256]{1,0:T(8,128)}, f32[256,256]{0,1:T(8,128)}) async-done(((f32[5120,256]{1,0:T(8,128)}, f32[256,256]{0,1:T(8,128)}), (f32[5120,256]{1,0:T(8,128)}, f32[256,256]{0,1:T(8,128)})) %all-reduce.16.cloned.1.call-update) | async-done | bytes 5505040 | tf_op jit(solution)/shard_map/psum | solution.py:40
  231.4 13.1 %fusion.26 = f32[256,256]{0,1:T(8,128)} fusion(f32[5120,256]{1,0:T(8,128)} %get-tuple-element.35), kind=kOutput, calls=%fused_computation.68 | convolution fusion | flops 4026531840 | bytes 5505024 | tf_op jit(solution)/shard_map/dot_general | solution.py:10
  245.3 11.7 %cholesky.130 = f32[128,128]{1,0:T(8,128)S(1)} custom-call(f32[128,128]{1,0:T(8,128)S(1)} %cholesky.194), custom_call_target="Cholesky" | custom-call | tf_op jit(solution)/shard_map/jit(cholesky)/cholesky | solution.py:20
  257.0 10.4 %custom-call.19 = f32[1,128,128]{1,2,0:T(8,128)} custom-call(f32[1,128,128]{2,1,0:T(8,128)S(1)} %get-tuple-element.44), custom_call_target="InvertDiagBlocksLowerTriangular" | custom-call | tf_op jit(solution)/shard_map/jit(cholesky)/cholesky | solution.py:20
  267.5 12.9 %all-reduce.10.cloned.1.call-done = f32[256,256]{0,1:T(8,128)} async-done(((f32[256,256]{0,1:T(8,128)}), f32[256,256]{0,1:T(8,128)}) %all-reduce.10.cloned.1.call-update) | async-done | bytes 262160 | tf_op jit(solution)/shard_map/psum | solution.py:42
  282.5 11.7 %cholesky.164 = f32[128,128]{1,0:T(8,128)S(1)} custom-call(f32[128,128]{1,0:T(8,128)S(1)} %cholesky.197), custom_call_target="Cholesky" | custom-call | tf_op jit(solution)/shard_map/jit(cholesky)/cholesky | solution.py:20
  294.2 10.0 %custom-call.20 = f32[1,128,128]{1,2,0:T(8,128)S(1)} custom-call(f32[1,128,128]{2,1,0:T(8,128)S(1)} %get-tuple-element.48), custom_call_target="InvertDiagBlocksLowerTriangular" | custom-call | tf_op jit(solution)/shard_map/jit(cholesky)/cholesky | solution.py:20
  304.7 11.7 %cholesky.181 = f32[128,128]{1,0:T(8,128)S(1)} custom-call(f32[128,128]{1,0:T(8,128)S(1)} %convolution_subtract_fusion.2), custom_call_target="Cholesky" | custom-call | tf_op jit(solution)/shard_map/jit(cholesky)/cholesky | solution.py:20
  318.5 4.0 while.3
  319.1 1.4 bitcast_dynamic-update-slice_fusion.5
  321.1 1.4 bitcast_dynamic-update-slice_fusion.5
  322.5 19.7 %custom-call.17 = f32[2,128,128]{1,2,0:T(8,128)S(1)} custom-call(f32[2,128,128]{2,1,0:T(8,128)S(1)} %get-tuple-element.18), custom_call_target="InvertDiagBlocksLowerTriangular" | custom-call | tf_op jit(solution)/shard_map/jit(_solve_triangular)/triangular_solve | solution.py:21
  342.2 5.4 fusion.21
  347.6 4.4 convolution_subtract_fusion
  352.1 2.4 convolution_convert_fusion
  355.6 13.7 %convolution_bitcast_fusion = f32[2560,256]{0,1:T(8,128)} fusion(bf16[2560,5120]{1,0:T(8,128)(2,1)} %param.4, bf16[128,5120]{1,0:T(8,128)(2,1)S(1)} %convolution_convert_fusion, bf16[128,5120]{1,0:T(8,128)(2,1)S(1)} %copy-done.4), kind=kOutput, calls=%fused_computation.7 | convolution fusion | flops 6716129280 | bytes 31457280 | tf_op jit(solution)/shard_map/dot_general | solution.py:45
  369.8 11.7 %cholesky.147 = f32[128,128]{1,0:T(8,128)S(1)} custom-call(f32[128,128]{1,0:T(8,128)S(1)} %convolution_subtract_fusion.3), custom_call_target="Cholesky" | custom-call | tf_op jit(solution)/shard_map/jit(cholesky)/cholesky | solution.py:20
  383.5 4.1 while.2
  386.3 1.3 bitcast_dynamic-update-slice_fusion.4
  387.6 20.3 %custom-call.16 = f32[2,128,128]{1,2,0:T(8,128)} custom-call(f32[2,128,128]{2,1,0:T(8,128)S(1)} %get-tuple-element.10), custom_call_target="InvertDiagBlocksLowerTriangular" | custom-call | tf_op jit(solution)/shard_map/jit(_solve_triangular)/triangular_solve | solution.py:21
  407.9 2.1 fusion.22
  410.1 2.2 convolution_subtract_fusion.1
  413.6 59.9 %all-reduce.12.cloned.1.call-done = f32[2560,256]{0,1:T(8,128)} async-done(((f32[2560,256]{0,1:T(8,128)}), f32[2560,256]{0,1:T(8,128)}) %all-reduce.12.cloned.1.call-update) | async-done | bytes 2621456 | tf_op jit(solution)/shard_map/psum | solution.py:46
  473.5 3.9 fusion.4
  477.3 53.1 %all-reduce.14.cloned.1.call-done = f32[256,256]{1,0:T(8,128)} async-done(((f32[256,256]{1,0:T(8,128)}), f32[256,256]{1,0:T(8,128)}) %all-reduce.14.cloned.1.call-update) | async-done | bytes 262160 | tf_op jit(solution)/shard_map/psum | solution.py:47
  530.4 3.5 convolution_convert_fusion.1
  533.9 22.9 %subtract_convert_fusion = bf16[2560,5120]{1,0:T(8,128)(2,1)} fusion(bf16[2560,5120]{1,0:T(8,128)(2,1)} %param.4, bf16[2560,256]{1,0:T(8,128)(2,1)} %convolution_convert_fusion.1, bf16[128,5120]{1,0:T(8,128)(2,1)} %copy-done.5, bf16[128,5120]{1,0:T(8,128)(2,1)} %get-tuple-element.51), kind=kOutput, calls=%fused_computation.4 | convolution fusion | flops 6755450880 | bytes 56360960 | tf_op jit(solution)/shard_map/dot_general | solution.py:55
  (66 shorter events, 13.8 us)
Async XLA Ops:
  7.2 1.7 copy-start
  7.2 122.2 %all-reduce.8.cloned.1.call-start = ((), (), s32[]{:S(2)}) async-start(), calls=%async_computation | async-start | bytes 5242880 | tf_op jit(solution)/shard_map/psum | solution.py:36
  22.4 1.3 copy-start.10
  22.5 208.9 %all-reduce.16.cloned.1.call-start = ((), (), s32[]{:S(2)}) async-start(), calls=%async_computation.4 | async-start | bytes 11010048 | tf_op jit(solution)/shard_map/psum | solution.py:40
  136.9 143.4 %all-reduce.10.cloned.1.call-start = ((), (), s32[]{:S(2)}) async-start(), calls=%async_computation.1 | async-start | bytes 524288 | tf_op jit(solution)/shard_map/psum | solution.py:42
  231.4 13.7 %copy-start.6 = (f32[256,256]{0,1:T(8,128)S(1)}, f32[256,256]{0,1:T(8,128)}, u32[]{:S(2)}) copy-start(f32[256,256]{0,1:T(8,128)} %get-tuple-element.36) | copy-start | bytes 786436
  244.6 228.9 %all-reduce.12.cloned.1.call-start = ((), (), s32[]{:S(2)}) async-start(), calls=%async_computation.2 | async-start | bytes 5242880 | tf_op jit(solution)/shard_map/psum | solution.py:46
  342.2 5.4 copy-start.2
  352.1 3.5 copy-start.4
  354.5 1.1 copy-start.5
  355.6 13.8 %copy-start.9 = (f32[1,128,128]{1,2,0:T(8,128)S(1)}, f32[1,128,128]{1,2,0:T(8,128)}, u32[]{:S(2)}) copy-start(f32[1,128,128]{1,2,0:T(8,128)} %custom-call.19) | copy-start | bytes 196612
  369.3 38.6 %copy-start.3 = (f32[2560,256]{1,0:T(8,128)S(1)}, f32[2560,256]{1,0:T(8,128)}, u32[]{:S(2)}) copy-start(f32[2560,256]{1,0:T(8,128)} %all-reduce.8.cloned.1.call-done) | copy-start | bytes 7864324
  369.3 161.1 %all-reduce.14.cloned.1.call-start = ((), (), s32[]{:S(2)}) async-start(), calls=%async_computation.3 | async-start | bytes 524288 | tf_op jit(solution)/shard_map/psum | solution.py:47
  410.0 2.2 copy-start.8
  533.9 22.9 %copy-start.7 = (f32[256,256]{1,0:T(8,128)S(1)}, f32[256,256]{1,0:T(8,128)}, u32[]{:S(2)}) copy-start(f32[256,256]{1,0:T(8,128)} %all-reduce.14.cloned.1.call-done) | copy-start | bytes 786436
  533.9 23.6 %copy-start.1 = (bf16[5120,256]{1,0:T(8,128)(2,1)S(1)}, bf16[5120,256]{1,0:T(8,128)(2,1)}, u32[]{:S(2)}) copy-start(bf16[5120,256]{1,0:T(8,128)(2,1)} %param.5) | copy-start | bytes 7864324
Sparse Core Ops, SparseCore 0:
  22.6 106.7 all-reduce.7
  137.1 94.2 all-reduce.15
  244.7 35.6 all-reduce.9
  369.4 103.9 all-reduce.11
  477.5 52.9 all-reduce.13
where the time goes:
time: 573 us; the launch traced here: 565 us
  waiting for transfers between devices  311 us (54%)
  matrix products  112 us (20%)
  other arithmetic  110 us (19%)
  between operations  17 us (3%)
  local copies, waits for them, and re-layouts  13.1 us (2%)
    psum x1, waiting for transfers between devices, body(): sketch_cols = lax.psum(sketch_cols, 'row')  94.2 us
    psum x1, waiting for transfers between devices, body(): sketch_rows = lax.psum(sketch_rows, 'col')  90.6 us
    another operation x12, other arithmetic, orthonormal(): lower_factor = jnp.linalg.cholesky(gram_total)  68.7 us
    psum x1, waiting for transfers between devices, body(): applied = lax.psum(applied, 'col')  59.9 us
    psum x1, waiting for transfers between devices, body(): core_matrix = lax.psum(core_part(basis_rows, applied), 'row')  53.1 us
    another operation x5, other arithmetic, orthonormal(): jax.scipy.linalg.solve_triangular(lower_factor, sketch.T, lower=True)  40 us
    dot_general x1, matrix products, body(): lax.dot_general(projected, basis_cols, (((1,), (1,)), ((), ())), preferre...  22.9 us
    dot_general x2, matrix products, gram_matrix(): lax.dot_general(sketch, sketch, (((0,), (0,)), ((), ())), precision=lax.P...  20.6 us
  transfers between devices with their start and end apart: 5, of which 5 were waited for; matrix products, arithmetic and copies ran while one was open for 14% of the time, Pallas kernels for 0%

commit v1 on v0

--- a/solution.py
+++ b/solution.py
@@ -33,7 +33,11 @@
 
 def body(front_matrix, right_samples, left_samples):
     sketch_rows = jnp.dot(front_matrix, right_samples, preferred_element_type=jnp.float32)
-    sketch_rows = lax.psum(sketch_rows, "col")
+    sketch_rows = sketch_rows
+    for hop in (1, 2):
+        sketch_rows = sketch_rows + lax.ppermute(
+            sketch_rows, "col", [(dev, dev ^ hop) for dev in range(4)]
+        )
     sketch_cols = lax.dot_general(
         front_matrix, left_samples, (((0,), (0,)), ((), ())), preferred_element_type=jnp.float32
     )

time: 573 us -> 642 us (1.12)
  waiting for transfers between devices: 311 us -> 372 us
    ppermute x0 -> x2, waiting for transfers between devices: none -> 155 us  [body(): lax.ppermute(sketch_rows, 'col', [(dev, dev ^ hop) for dev in range(4)])]
    psum x1 -> x0, waiting for transfers between devices: 90.6 us -> none  [body(): sketch_rows = lax.psum(sketch_rows, 'col')]
  transfers between devices with their start and end apart: 5 -> 6, of which waited for: 5 -> 6; matrix products, arithmetic and copies ran while one was open for 14% -> 13% of each run, Pallas kernels for 0% -> 0%
where the time goes in v1:
time: 642 us; the launch traced here: 633 us
  waiting for transfers between devices  372 us (58%)
  other arithmetic  114 us (18%)
  matrix products  109 us (17%)
  between operations  17.1 us (3%)
  local copies, waits for them, and re-layouts  13.5 us (2%)
  starting transfers between devices  6.78 us (1%)
    ppermute x2, waiting for transfers between devices, body(): lax.ppermute(sketch_rows, 'col', [(dev, dev ^ hop) for dev in range(4)])  155 us
    psum x1, waiting for transfers between devices, body(): sketch_cols = lax.psum(sketch_cols, 'row')  92.6 us
    another operation x12, other arithmetic, orthonormal(): lower_factor = jnp.linalg.cholesky(gram_total)  68.8 us
    psum x1, waiting for transfers between devices, body(): applied = lax.psum(applied, 'col')  58.7 us
    psum x1, waiting for transfers between devices, body(): core_matrix = lax.psum(core_part(basis_rows, applied), 'row')  53.1 us
    another operation x5, other arithmetic, orthonormal(): jax.scipy.linalg.solve_triangular(lower_factor, sketch.T, lower=True)  40 us
    dot_general x1, matrix products, body(): lax.dot_general(projected, basis_cols, (((1,), (1,)), ((), ())), preferre...  22.9 us
    another operation x6, matrix products, orthonormal(): jax.scipy.linalg.solve_triangular(lower_factor, sketch.T, lower=True)  18.8 us
  transfers between devices with their start and end apart: 6, of which 6 were waited for; matrix products, arithmetic and copies ran while one was open for 13% of the time, Pallas kernels for 0%

profile of v1, /device:TPU:0, one launch (start us, length us, event | category | flops | bytes accessed | tf_op | source)
XLA Modules:
  0.0 633.3 jit_solution(5908044176676782673)
XLA Ops:
  8.9 12.3 %fusion.26 = f32[2560,256]{1,0:T(8,128)S(1)} fusion(bf16[2560,5120]{1,0:T(8,128)(2,1)} %param.4, bf16[5120,256]{1,0:T(8,128)(2,1)S(1)} %copy-done), kind=kOutput, calls=%fused_computation.69 | convolution fusion | flops 6710886400 | bytes 31457280 | tf_op jit(solution)/shard_map/dot_general | solution.py:35
  21.2 3.1 collective-permute-start
  24.3 56.9 %collective-permute-done = f32[2560,256]{1,0:T(8,128)S(1)} collective-permute-done((f32[2560,256]{1,0:T(8,128)S(1)}, f32[2560,256]{1,0:T(8,128)S(1)}, u32[]{:S(2)}, u32[]{:S(2)}) %collective-permute-start) | collective-permute-done | bytes 2621472 | tf_op jit(solution)/shard_map/ppermute | solution.py:38
  81.5 2.8 collective-permute-start.1
  84.3 14.7 %fusion.27 = f32[5120,256]{1,0:T(8,128)} fusion(bf16[2560,5120]{1,0:T(8,128)(2,1)} %param.4, bf16[2560,256]{1,0:T(8,128)(2,1)S(1)} %copy-done.12), kind=kOutput, calls=%fused_computation.70 | convolution fusion | flops 6710886400 | bytes 32768000 | tf_op jit(solution)/shard_map/dot_general | solution.py:41
  99.0 97.7 %collective-permute-done.1 = f32[2560,256]{1,0:T(8,128)S(1)} collective-permute-done((f32[2560,256]{1,0:T(8,128)S(1)}, f32[2560,256]{1,0:T(8,128)S(1)}, u32[]{:S(2)}, u32[]{:S(2)}) %collective-permute-start.1) | collective-permute-done | bytes 2621472 | tf_op jit(solution)/shard_map/ppermute | solution.py:38
  198.2 5.2 fusion.4
  203.7 3.6 add_bitcast_fusion
  207.3 92.6 %all-reduce.13.cloned.1.call-done = (f32[5120,256]{1,0:T(8,128)}, f32[256,256]{0,1:T(8,128)}) async-done(((f32[5120,256]{1,0:T(8,128)}, f32[256,256]{0,1:T(8,128)}), (f32[5120,256]{1,0:T(8,128)}, f32[256,256]{0,1:T(8,128)})) %all-reduce.13.cloned.1.call-update) | async-done | bytes 5505040 | tf_op jit(solution)/shard_map/psum | solution.py:44
  299.9 13.1 %fusion.28 = f32[256,256]{0,1:T(8,128)} fusion(f32[5120,256]{1,0:T(8,128)} %get-tuple-element.35), kind=kOutput, calls=%fused_computation.71 | convolution fusion | flops 4026531840 | bytes 5505024 | tf_op jit(solution)/shard_map/dot_general | solution.py:10
  313.8 11.7 %cholesky.130 = f32[128,128]{1,0:T(8,128)S(1)} custom-call(f32[128,128]{1,0:T(8,128)S(1)} %cholesky.194), custom_call_target="Cholesky" | custom-call | tf_op jit(solution)/shard_map/jit(cholesky)/cholesky | solution.py:20
  325.5 10.4 %custom-call.19 = f32[1,128,128]{1,2,0:T(8,128)} custom-call(f32[1,128,128]{2,1,0:T(8,128)S(1)} %get-tuple-element.44), custom_call_target="InvertDiagBlocksLowerTriangular" | custom-call | tf_op jit(solution)/shard_map/jit(cholesky)/cholesky | solution.py:20
  336.0 12.9 %all-reduce.7.cloned.1.call-done = f32[256,256]{0,1:T(8,128)} async-done(((f32[256,256]{0,1:T(8,128)}), f32[256,256]{0,1:T(8,128)}) %all-reduce.7.cloned.1.call-update) | async-done | bytes 262160 | tf_op jit(solution)/shard_map/psum | solution.py:46
  351.0 11.7 %cholesky.164 = f32[128,128]{1,0:T(8,128)S(1)} custom-call(f32[128,128]{1,0:T(8,128)S(1)} %cholesky.197), custom_call_target="Cholesky" | custom-call | tf_op jit(solution)/shard_map/jit(cholesky)/cholesky | solution.py:20
  362.8 10.0 %custom-call.20 = f32[1,128,128]{1,2,0:T(8,128)S(1)} custom-call(f32[1,128,128]{2,1,0:T(8,128)S(1)} %get-tuple-element.48), custom_call_target="InvertDiagBlocksLowerTriangular" | custom-call | tf_op jit(solution)/shard_map/jit(cholesky)/cholesky | solution.py:20
  373.2 11.7 %cholesky.181 = f32[128,128]{1,0:T(8,128)S(1)} custom-call(f32[128,128]{1,0:T(8,128)S(1)} %convolution_subtract_fusion.1), custom_call_target="Cholesky" | custom-call | tf_op jit(solution)/shard_map/jit(cholesky)/cholesky | solution.py:20
  387.1 4.0 while.3
  391.1 19.7 %custom-call.17 = f32[2,128,128]{1,2,0:T(8,128)S(1)} custom-call(f32[2,128,128]{2,1,0:T(8,128)S(1)} %get-tuple-element.18), custom_call_target="InvertDiagBlocksLowerTriangular" | custom-call | tf_op jit(solution)/shard_map/jit(_solve_triangular)/triangular_solve | solution.py:21
  410.8 5.4 fusion.24
  416.2 4.4 convolution_subtract_fusion
  420.6 2.4 convolution_convert_fusion
  424.1 13.7 %convolution_bitcast_fusion = f32[2560,256]{0,1:T(8,128)} fusion(bf16[2560,5120]{1,0:T(8,128)(2,1)} %param.4, bf16[128,5120]{1,0:T(8,128)(2,1)S(1)} %convolution_convert_fusion, bf16[128,5120]{1,0:T(8,128)(2,1)S(1)} %copy-done.6), kind=kOutput, calls=%fused_computation.7 | convolution fusion | flops 6716129280 | bytes 31457280 | tf_op jit(solution)/shard_map/dot_general | solution.py:49
  438.3 11.7 %cholesky.147 = f32[128,128]{1,0:T(8,128)S(1)} custom-call(f32[128,128]{1,0:T(8,128)S(1)} %convolution_subtract_fusion.2), custom_call_target="Cholesky" | custom-call | tf_op jit(solution)/shard_map/jit(cholesky)/cholesky | solution.py:20
  452.1 4.2 while.2
  456.4 20.3 %custom-call.16 = f32[2,128,128]{1,2,0:T(8,128)} custom-call(f32[2,128,128]{2,1,0:T(8,128)S(1)} %get-tuple-element.10), custom_call_target="InvertDiagBlocksLowerTriangular" | custom-call | tf_op jit(solution)/shard_map/jit(_solve_triangular)/triangular_solve | solution.py:21
  476.7 2.2 fusion.25
  478.9 2.2 fusion.12
  483.3 58.7 %all-reduce.9.cloned.1.call-done = f32[2560,256]{0,1:T(8,128)} async-done(((f32[2560,256]{0,1:T(8,128)}), f32[2560,256]{0,1:T(8,128)}) %all-reduce.9.cloned.1.call-update) | async-done | bytes 2621456 | tf_op jit(solution)/shard_map/psum | solution.py:50
  541.9 4.1 fusion.6
  546.1 53.1 %all-reduce.11.cloned.1.call-done = f32[256,256]{1,0:T(8,128)} async-done(((f32[256,256]{1,0:T(8,128)}), f32[256,256]{1,0:T(8,128)}) %all-reduce.11.cloned.1.call-update) | async-done | bytes 262160 | tf_op jit(solution)/shard_map/psum | solution.py:51
  599.1 3.5 convolution_convert_fusion.1
  602.6 22.9 %subtract_convert_fusion = bf16[2560,5120]{1,0:T(8,128)(2,1)} fusion(bf16[2560,5120]{1,0:T(8,128)(2,1)} %param.4, bf16[2560,256]{1,0:T(8,128)(2,1)} %convolution_convert_fusion.1, bf16[128,5120]{1,0:T(8,128)(2,1)} %copy-done.7, bf16[128,5120]{1,0:T(8,128)(2,1)} %get-tuple-element.51), kind=kOutput, calls=%fused_computation.4 | convolution fusion | flops 6755450880 | bytes 56360960 | tf_op jit(solution)/shard_map/dot_general | solution.py:59
  (73 shorter events, 21.2 us)
Async XLA Ops:
  7.2 1.7 copy-start
  7.2 292.7 %all-reduce.13.cloned.1.call-start = ((), (), s32[]{:S(2)}) async-start(), calls=%async_computation.3 | async-start | bytes 11010048 | tf_op jit(solution)/shard_map/psum | solution.py:44
  21.2 63.2 %copy-start.12 = (bf16[2560,256]{1,0:T(8,128)(2,1)S(1)}, bf16[2560,256]{1,0:T(8,128)(2,1)}, u32[]{:S(2)}) copy-start(bf16[2560,256]{1,0:T(8,128)(2,1)} %param.6) | copy-start | bytes 3932164
  21.2 60.0 %collective-permute-start = (f32[2560,256]{1,0:T(8,128)S(1)}, f32[2560,256]{1,0:T(8,128)S(1)}, u32[]{:S(2)}, u32[]{:S(2)}) collective-permute-start(f32[2560,256]{1,0:T(8,128)S(1)} %fusion.26), channel_id=1, source_target_pairs={{0,1},{1,0},{2,3},{3,2},{4,5},{5,4},{6,7},{7,6},{8,9},{9,8},{10,11... | collective-permute-start | bytes 7864328 | tf_op jit(solution)/shard_map/ppermute | solution.py:38
  81.5 115.2 %collective-permute-start.1 = (f32[2560,256]{1,0:T(8,128)S(1)}, f32[2560,256]{1,0:T(8,128)S(1)}, u32[]{:S(2)}, u32[]{:S(2)}) collective-permute-start(f32[2560,256]{1,0:T(8,128)S(1)} %add.38), channel_id=1, source_target_pairs={{0,2},{1,3},{2,0},{3,1},{4,6},{5,7},{6,4},{7,5},{8,10},{9,11},{10,... | collective-permute-start | bytes 7864328 | tf_op jit(solution)/shard_map/ppermute | solution.py:38
  196.7 1.5 copy-start.4
  203.4 145.5 %all-reduce.7.cloned.1.call-start = ((), (), s32[]{:S(2)}) async-start(), calls=%async_computation | async-start | bytes 524288 | tf_op jit(solution)/shard_map/psum | solution.py:46
  299.9 13.7 %copy-start.8 = (f32[256,256]{0,1:T(8,128)S(1)}, f32[256,256]{0,1:T(8,128)}, u32[]{:S(2)}) copy-start(f32[256,256]{0,1:T(8,128)} %get-tuple-element.36) | copy-start | bytes 786436
  313.1 228.9 %all-reduce.9.cloned.1.call-start = ((), (), s32[]{:S(2)}) async-start(), calls=%async_computation.1 | async-start | bytes 5242880 | tf_op jit(solution)/shard_map/psum | solution.py:50
  410.8 5.4 copy-start.2
  420.6 3.5 copy-start.6
  423.0 1.1 copy-start.7
  424.1 13.8 %copy-start.11 = (f32[1,128,128]{1,2,0:T(8,128)S(1)}, f32[1,128,128]{1,2,0:T(8,128)}, u32[]{:S(2)}) copy-start(f32[1,128,128]{1,2,0:T(8,128)} %custom-call.19) | copy-start | bytes 196612
  437.8 38.9 %copy-start.3 = (f32[256,2560]{0,1:T(8,128)S(1)}, f32[256,2560]{0,1:T(8,128)}, u32[]{:S(2)}) copy-start(f32[256,2560]{0,1:T(8,128)} %add_bitcast_fusion) | copy-start | bytes 7864324
  437.8 161.3 %all-reduce.11.cloned.1.call-start = ((), (), s32[]{:S(2)}) async-start(), calls=%async_computation.2 | async-start | bytes 524288 | tf_op jit(solution)/shard_map/psum | solution.py:51
  476.7 4.4 copy-start.10
  483.3 115.8 %copy-start.5 = (bf16[128,2560]{1,0:T(8,128)(2,1)S(1)}, bf16[128,2560]{1,0:T(8,128)(2,1)}, u32[]{:S(2)}) copy-start(bf16[128,2560]{1,0:T(8,128)(2,1)} %convolution_convert_fusion.2) | copy-start | bytes 1966084
  602.6 22.9 %copy-start.9 = (f32[256,256]{1,0:T(8,128)S(1)}, f32[256,256]{1,0:T(8,128)}, u32[]{:S(2)}) copy-start(f32[256,256]{1,0:T(8,128)} %all-reduce.11.cloned.1.call-done) | copy-start | bytes 786436
  602.6 23.6 %copy-start.1 = (bf16[5120,256]{1,0:T(8,128)(2,1)S(1)}, bf16[5120,256]{1,0:T(8,128)(2,1)}, u32[]{:S(2)}) copy-start(bf16[5120,256]{1,0:T(8,128)(2,1)} %param.5) | copy-start | bytes 7864324
Sparse Core Ops, SparseCore 0:
  203.6 96.2 all-reduce.12
  313.2 35.6 all-reduce.6
  437.9 103.9 all-reduce.8
  546.2 52.8 all-reduce.10
